TPU v7x, 32 devices: a whole 2x2x4 slice. The times are simulated.
32 devices in a mesh: shard: 2 (over y), tensor: 4 (over z), section: 4 (over x, core).
Axes of the slice: x: 2, y: 2, z: 4, core: 2. Of those that a mesh axis runs over, the one named last changes fastest.
Arguments:
- xin: bfloat16 [4, 16384, 768], P(None, ('shard', 'tensor', 'section')), may hold values from -6 to 6
- dout: bfloat16 [4, 16384, 768], P(None, ('shard', 'tensor', 'section')), may hold values from -6 to 6
- weights: bfloat16 [4, 768, 768], P(None, ('tensor', 'section')), may hold values from -0.21875 to 0.21875
- slot_block: int32 [8], replicated, may hold values from -1 to 3, as said below
- left_stat: float32 [8, 768, 768], P('shard', ('tensor', 'section')), may hold values from -1 to 10, as said below
- right_stat: float32 [8, 768, 768], P('shard', ('tensor', 'section')), may hold values from -1 to 10, as said below
- left_root: float32 [8, 768, 768], P('shard', ('tensor', 'section')), may hold values from -1 to 10, as said below
- right_root: float32 [8, 768, 768], P('shard', ('tensor', 'section')), may hold values from -1 to 10, as said below
- first_moment: float32 [8, 768, 768], P('shard', ('tensor', 'section')), may hold values from -0.3 to 0.3
- second_moment: float32 [8, 768, 768], P('shard', ('tensor', 'section')), may hold values from 0.001 to 0.01
Outputs:
- new_weights: bfloat16 [4, 768, 768], P(None, ('tensor', 'section'))
- new_left: float32 [8, 768, 768], P('shard', ('tensor', 'section'))
- new_right: float32 [8, 768, 768], P('shard', ('tensor', 'section'))
- new_first: float32 [8, 768, 768], P('shard', ('tensor', 'section'))
- new_second: float32 [8, 768, 768], P('shard', ('tensor', 'section'))
Inputs may be any that keep to these rules, and one draw needn't show every extreme that they name: `slot_block`: every block 0 to 3 stands in exactly one slot; slots 4 s to 4 s + 3 belong to shard index s; some shard index holds two blocks and none holds more; the other slots hold -1. `left_stat`: each slot is a symmetric positive definite matrix. `right_stat`: each slot is a symmetric positive definite matrix. `left_root`: each slot is a symmetric positive definite matrix. `right_root`: each slot is a symmetric positive definite matrix.
All inputs are finite; a program needn't handle non-finite values.
Results may differ from a plain program's by a relative error of at most 0.00045.
Values may be sent and summed in bfloat16 or wider, within the bound.
No kernel may reach another device: no remote copies, remote signals or barrier semaphores. Data moves between devices by JAX's collectives and lax.ppermute only.
A program may use at most 128 MiB of HBM per device.

v0:
```python
import math
import jax
import jax.numpy as jnp
from jax import lax
from jax.sharding import PartitionSpec as P


def spread(value, axis, source):
    kept = jnp.where(lax.axis_index(axis) == source, value, 0).astype(value.dtype)
    return lax.psum(kept, axis)


def absorb_slot(mine_rows, root_rows, portion, col_first):
    highest = lax.Precision.HIGHEST
    row_count = mine_rows.shape[0]
    block_part = jnp.dot(mine_rows, portion.T, precision=highest)
    own_cols = lax.dynamic_slice_in_dim(portion, col_first, row_count, 1)
    right_gram = jnp.dot(own_cols.T, portion, precision=highest)
    left_prod = jnp.dot(root_rows, portion, precision=highest)
    return (block_part, right_gram, left_prod)


def apply_slot(prod_rows, portion):
    return jnp.dot(prod_rows, portion, precision=lax.Precision.HIGHEST)


def on_device(
    xin,
    dout,
    weights,
    slot_block,
    left_stat,
    right_stat,
    left_root,
    right_root,
    first_moment,
    second_moment,
):
    block_count, tok_count, block_size = xin.shape
    slot_count, row_count = (left_stat.shape[0], left_stat.shape[1])
    group_count = lax.axis_size(("tensor", "section"))
    shard_count = lax.axis_size("shard")
    factor = 1.0 / math.sqrt(tok_count * shard_count * group_count * block_size)
    pieces_out = []
    for grad_member in range(block_count):
        cols = xin[grad_member]
        pieces_out.append(
            jnp.einsum("tr,tc->rc", cols, dout[grad_member], preferred_element_type=jnp.float32)
        )
    partial_rows = lax.psum_scatter(
        jnp.concatenate(pieces_out, axis=1) * factor,
        ("tensor", "section"),
        scatter_dimension=0,
        tiled=True,
    )
    grad_rows = lax.psum(partial_rows, "shard")
    shard_idx = lax.axis_index("shard")
    group_idx = lax.axis_index(("tensor", "section"))
    my_slots = lax.dynamic_slice_in_dim(slot_block, shard_idx * slot_count, slot_count)
    valid = my_slots >= 0
    picks = jnp.maximum(my_slots, 0)
    grad_three = grad_rows.reshape(row_count, block_count, block_size)
    mine = jnp.moveaxis(jnp.take(grad_three, picks, axis=1), 1, 0)
    col_first = group_idx * row_count
    zeros_rows = jnp.zeros((slot_count, row_count, block_size), jnp.float32)
    totals = (zeros_rows, zeros_rows, zeros_rows)
    portion = lax.all_gather(mine, ("tensor", "section"), axis=1, tiled=True)
    lefts = []
    rights = []
    prods = []
    for slot_pos in range(slot_count):
        current = (totals[0][slot_pos], totals[1][slot_pos], totals[2][slot_pos])
        result = lax.cond(
            valid[slot_pos],
            lambda values: absorb_slot(
                mine[slot_pos], left_root[slot_pos], portion[slot_pos], col_first
            ),
            lambda values: values,
            current,
        )
        lefts.append(result[0])
        rights.append(result[1])
        prods.append(result[2])
    left_gram = jnp.stack(lefts)
    right_gram = jnp.stack(rights)
    left_prod = jnp.stack(prods)
    apply_portion = lax.all_gather(right_root, ("tensor", "section"), axis=1, tiled=True)
    outputs = []
    for apply_slot_pos in range(slot_count):
        outputs.append(
            lax.cond(
                valid[apply_slot_pos],
                lambda values: apply_slot(left_prod[apply_slot_pos], apply_portion[apply_slot_pos]),
                lambda values: values,
                zeros_rows[apply_slot_pos],
            )
        )
    direction = jnp.stack(outputs)
    moment_one = 0.9 * first_moment + 0.1 * mine
    moment_two = 0.999 * second_moment + 0.001 * mine * mine
    adam = moment_one / (jnp.sqrt(moment_two) + 1e-08)
    adam_sq, dir_sq = lax.psum(
        (jnp.sum(adam * adam, axis=(1, 2)), jnp.sum(direction * direction, axis=(1, 2))),
        ("tensor", "section"),
    )
    graft = jnp.sqrt(adam_sq) / (jnp.sqrt(dir_sq) + 1e-06)
    mask = valid[:, None, None]
    new_left = jnp.where(mask, 0.5 * left_stat + 0.5 * left_gram, left_stat)
    new_right = jnp.where(mask, 0.5 * right_stat + 0.5 * right_gram, right_stat)
    new_first = jnp.where(mask, moment_one, first_moment)
    new_second = jnp.where(mask, moment_two, second_moment)
    my_weights = jnp.take(weights, picks, axis=0)
    new_rows = (my_weights.astype(jnp.float32) - 0.05 * graft[:, None, None] * direction).astype(
        jnp.bfloat16
    )
    slot_ids = jnp.arange(slot_block.shape[0], dtype=jnp.int32)
    holders = [
        jnp.sum(slot_ids * (slot_block == member).astype(jnp.int32))
        for member in range(block_count)
    ]
    published = []
    for member in range(block_count):
        owner = holders[member] // slot_count
        within = holders[member] % slot_count
        chosen = lax.dynamic_index_in_dim(new_rows, within, 0, keepdims=False)
        published.append(spread(chosen, "shard", owner))
    new_weights = jnp.stack(published)
    return (new_weights, new_left, new_right, new_first, new_second)


def solution(mesh):
    placed = (
        P(None, ("shard", "tensor", "section"), None),
        P(None, ("shard", "tensor", "section"), None),
        P(None, ("tensor", "section"), None),
        P(),
        P("shard", ("tensor", "section"), None),
        P("shard", ("tensor", "section"), None),
        P("shard", ("tensor", "section"), None),
        P("shard", ("tensor", "section"), None),
        P("shard", ("tensor", "section"), None),
        P("shard", ("tensor", "section"), None),
    )
    return jax.shard_map(
        on_device,
        mesh=mesh,
        in_specs=placed,
        out_specs=(
            P(None, ("tensor", "section"), None),
            P("shard", ("tensor", "section"), None),
            P("shard", ("tensor", "section"), None),
            P("shard", ("tensor", "section"), None),
            P("shard", ("tensor", "section"), None),
        ),
        check_vma=False,
    )
```

profile of v0, /device:TPU:0, one launch (start us, length us, event | category | flops | bytes accessed | tf_op | source)
XLA Modules:
  0.0 413.0 jit_solution(5907693126761822649)
XLA Ops:
  7.2 2.4 fusion.108
  9.6 2.1 fusion.111
  12.6 0.8 fusion.117
  13.4 4.1 maximum_multiply_fusion
  17.5 9.7 %copy.20 = f32[768,3072]{1,0:T(8,128)} copy(f32[768,3072]{0,1:T(8,128)} %maximum_multiply_fusion) | data formatting | bytes 18874368
  27.2 114.2 %reduce-scatter.4.cloned.1.call-done = f32[48,3072]{1,0:T(8,128)} async-done(((f32[768,3072]{1,0:T(8,128)}), f32[48,3072]{1,0:T(8,128)}) %reduce-scatter.4.cloned.1.call-update) | async-done | bytes 589840
  141.4 1.5 copy.21
  142.9 1.3 copy.17
  144.4 29.8 %all-reduce.5.cloned.1.call-done = f32[48,4,768]{2,0,1:T(8,128)} async-done(((f32[48,4,768]{2,0,1:T(8,128)}), f32[48,4,768]{2,0,1:T(8,128)}) %all-reduce.5.cloned.1.call-update) | async-done | bytes 589840 | tf_op jit(solution)/shard_map/psum | solution.py:56
  174.2 1.6 gather_fusion.1
  175.9 1.2 fusion.134
  192.7 66.0 %all-gather.5.cloned.1.call-done = f32[4,768,768]{2,1,0:T(8,128)} async-done(((f32[4,48,768]{2,1,0:T(8,128)}), f32[4,768,768]{2,1,0:T(8,128)}) %all-gather.5.cloned.1.call-update) | async-done | bytes 9437200 | tf_op jit(solution)/shard_map/all_gather | solution.py:67
  258.8 11.2 %conditional.10 = (f32[48,768]{1,0:T(8,128)S(1)}, f32[1,48,768]{2,1,0:T(8,128)S(1)}, f32[1,48,768]{2,1,0:T(8,128)S(1)}) conditional(s32[]{:T(128)} %bitcast.42, () %tuple.93, (f32[4,48,768]{2,1,0:T(8,128)}, f32[4,768,768]{2,1,0:T(8,128)}, f32[4,48,768]{2,1,0:T(8,128)}, s32[]{:T(128)}) %tuple.90), branch_computations={%region_9.10_spmd, %region_10.11_spmd} | conditional | flops 1019215872 | bytes 12927038 | solution.py:73
  259.0 1.8 slice.65
  260.8 1.7 fusion.36
  262.5 3.3 fusion.31
  265.7 4.2 %fusion.33 = f32[1,48,768]{2,1,0:T(8,128)S(1)} fusion(f32[4,48,768]{2,1,0:T(8,128)} %get-tuple-element.80, f32[4,768,768]{2,1,0:T(8,128)} %get-tuple-element.79), kind=kOutput, calls=%fused_computation.29 | convolution fusion | flops 339738624 | bytes 2654208 | tf_op jit(solution)/shard_map/cond/branch_1_fun/dot_general | solution.py:16
  271.4 10.8 %conditional.14 = (f32[48,768]{1,0:T(8,128)S(1)}, f32[1,48,768]{2,1,0:T(8,128)S(1)}, f32[1,48,768]{2,1,0:T(8,128)S(1)}) conditional(s32[]{:T(128)} %bitcast.44, () %tuple.99, (f32[4,48,768]{2,1,0:T(8,128)}, f32[4,768,768]{2,1,0:T(8,128)}, f32[4,48,768]{2,1,0:T(8,128)}, s32[]{:T(128)}) %tuple.90), branch_computations={%region_17.18_spmd, %region_18.19_spmd} | conditional | flops 1019215872 | bytes 12927038 | solution.py:73
  271.4 1.8 slice.73
  273.3 1.7 fusion.90
  275.0 3.3 fusion.85
  278.2 4.0 fusion.87
  282.3 58.2 %all-gather.3.cloned.1.call-done = f32[4,768,768]{2,1,0:T(8,128)} async-done(((f32[4,48,768]{2,1,0:T(8,128)}), f32[4,768,768]{2,1,0:T(8,128)}) %all-gather.3.cloned.1.call-update) | async-done | bytes 9437200 | tf_op jit(solution)/shard_map/all_gather | solution.py:87
  340.5 3.2 conditional.11
  340.5 3.2 fusion.51
  343.8 0.8 copy-done.13
  344.6 3.2 conditional.15
  344.6 3.2 fusion.105
  348.0 3.3 fusion.133
  351.3 30.8 %all-reduce = (f32[4]{0:T(128)S(1)}, f32[4]{0:T(128)S(1)}) all-reduce(f32[4]{0:T(128)S(1)} %multiply_reduce_fusion, f32[4]{0:T(128)S(1)} %get-tuple-element.140), channel_id=1, replica_groups=mesh['shard'=2,'tensor'=4,'section'=4] {'tensor','section'}, use_global_device_ids=true, to_apply=%region_22.23 | all-reduce | flops 8 | bytes 64 | tf_op jit(solution)/shard_map/psum | solution.py:102
  383.1 21.7 %all-reduce.7.cloned.1.call-done = (bf16[1,48,768]{2,1,0:T(8,128)(2,1)}, bf16[1,48,768]{2,1,0:T(8,128)(2,1)}, bf16[1,48,768]{2,1,0:T(8,128)(2,1)}, bf16[1,48,768]{2,1,0:T(8,128)(2,1)}) async-done(((bf16[1,48,768]{2,1,0:T(8,128)(2,1)}, bf16[1,48,768]{2,1,0:T(8,128)(2,1)}, bf16[1,48,768]{2,1,0:T(8,128)(2,1)}, bf16[1,48,768]{2,1,0:T(8,128)(2,1)}), (bf16[1,48,768]{2,1,0:T(8,128)(2,1)}, ...) | async-done | bytes 294928 | tf_op jit(solution)/shard_map/psum | solution.py:10
  404.7 1.7 pad_maximum_fusion.1
  (61 shorter events, 6.4 us)
Async XLA Ops:
  7.2 184.8 %copy-start = (bf16[4,48,768]{2,1,0:T(8,128)(2,1)S(1)}, bf16[4,48,768]{2,1,0:T(8,128)(2,1)}, u32[]{:S(2)}) copy-start(bf16[4,48,768]{2,1,0:T(8,128)(2,1)} %param.28) | copy-start | bytes 884740
  7.2 2.4 copy-start.3
  7.2 134.2 %reduce-scatter.4.cloned.1.call-start = ((), (), s32[]{:S(2)}) async-start(), calls=%async_computation.4 | async-start | bytes 10027008
  9.6 2.1 copy-start.4
  27.2 117.1 %copy-start.14 = (s32[8]{0:T(128)S(1)}, s32[8]{0:T(128)}, u32[]{:S(2)}) copy-start(s32[8]{0:T(128)} %param.29) | copy-start | bytes 100
  27.2 147.0 %all-reduce.5.cloned.1.call-start = ((), (), s32[]{:S(2)}) async-start(), calls=%async_computation.1 | async-start | bytes 1179648 | tf_op jit(solution)/shard_map/psum | solution.py:56
  142.9 32.9 %copy-start.5 = (f32[4,48,768]{2,1,0:T(8,128)S(1)}, f32[4,48,768]{2,1,0:T(8,128)}, u32[]{:S(2)}) copy-start(f32[4,48,768]{2,1,0:T(8,128)} %param.35) | copy-start | bytes 1769476
  144.2 114.5 %all-gather.5.cloned.1.call-start = ((), (), s32[]{:S(2)}) async-start(), calls=%async_computation.3 | async-start | bytes 10027008 | tf_op jit(solution)/shard_map/all_gather | solution.py:67
  177.1 163.4 %all-gather.3.cloned.1.call-start = ((), (), s32[]{:S(2)}) async-start(), calls=%async_computation.2 | async-start | bytes 10027008 | tf_op jit(solution)/shard_map/all_gather | solution.py:87
  177.7 227.1 %all-reduce.7.cloned.1.call-start = ((), (), s32[]{:S(2)}) async-start(), calls=%async_computation.5 | async-start | bytes 589824 | tf_op jit(solution)/shard_map/psum | solution.py:10
  270.0 0.7 copy-start.7
  270.7 0.7 copy-start.8
  270.7 0.7 copy-start.9
  282.3 61.4 %copy-start.10 = (f32[1,48,768]{2,1,0:T(8,128)}, f32[1,48,768]{2,1,0:T(8,128)S(1)}, u32[]{:S(2)}) copy-start(f32[1,48,768]{2,1,0:T(8,128)S(1)} %get-tuple-element.120) | copy-start | bytes 442372
  282.3 61.4 %copy-start.11 = (f32[1,48,768]{2,1,0:T(8,128)}, f32[1,48,768]{2,1,0:T(8,128)S(1)}, u32[]{:S(2)}) copy-start(f32[1,48,768]{2,1,0:T(8,128)S(1)} %get-tuple-element.124) | copy-start | bytes 442372
  282.3 61.4 %copy-start.12 = (f32[48,768]{1,0:T(8,128)}, f32[48,768]{1,0:T(8,128)S(1)}, u32[]{:S(2)}) copy-start(f32[48,768]{1,0:T(8,128)S(1)} %get-tuple-element.116) | copy-start | bytes 442372
  343.7 0.9 copy-start.13
  343.8 4.2 %copy-start.2 = (f32[4,48,768]{2,1,0:T(8,128)S(1)}, f32[4,48,768]{2,1,0:T(8,128)}, u32[]{:S(2)}) copy-start(f32[4,48,768]{2,1,0:T(8,128)} %get-tuple-element.136) | copy-start | bytes 1769476
  343.8 4.2 %copy-start.6 = (f32[4,48,768]{2,1,0:T(8,128)S(1)}, f32[4,48,768]{2,1,0:T(8,128)}, u32[]{:S(2)}) copy-start(f32[4,48,768]{2,1,0:T(8,128)} %param.34) | copy-start | bytes 1769476
  348.0 58.5 %copy-start.1 = (bf16[4,48,768]{2,1,0:T(8,128)(2,1)S(1)}, bf16[4,48,768]{2,1,0:T(8,128)(2,1)}, u32[]{:S(2)}) copy-start(bf16[4,48,768]{2,1,0:T(8,128)(2,1)} %param.28) | copy-start | bytes 884740
Sparse Core Ops, SparseCore 0:
  27.3 114.0 reduce-scatter.3
  144.4 29.7 all-reduce.4
  177.2 81.4 all-gather.4
  260.9 79.5 all-gather.2
  383.2 21.4 all-reduce.6
where the time goes:
time: 414 us; the launch traced here: 413 us
  waiting for transfers between devices  290 us (70%)
  blocking collectives  30.8 us (7%)
  matrix products  30.6 us (7%)
  between operations  27.2 us (7%)
  local copies, waits for them, and re-layouts  21.3 us (5%)
  other arithmetic  12.2 us (3%)
    unnamed x6, waiting for transfers between devices  115 us
    all_gather x1, waiting for transfers between devices, on_device(): portion = lax.all_gather(mine, ('tensor', 'section'), axis=1, tiled=True)  66 us
    all_gather x1, waiting for transfers between devices, on_device(): lax.all_gather(right_root, ('tensor', 'section'), axis=1, tiled=True)  58.2 us
    psum x1, blocking collectives, on_device(): lax.psum((jnp.sum(adam * adam, axis=(1, 2)), jnp.sum(direction * directio...  30.8 us
    psum x1, waiting for transfers between devices, on_device(): grad_rows = lax.psum(partial_rows, 'shard')  29.8 us
    psum x1, waiting for transfers between devices, spread(): return lax.psum(kept, axis)  21.7 us
    unnamed x32, local copies, waits for them, and re-layouts  13.4 us
    dot_general x2, matrix products, absorb_slot(): block_part = jnp.dot(mine_rows, portion.T, precision=highest)  8.3 us
  transfers between devices with their start and end apart: 5, of which 5 were waited for; matrix products, arithmetic and copies ran while one was open for 6% of the time, Pallas kernels for 0%

commit v1 on v0

--- a/solution.py
+++ b/solution.py
@@ -100,8 +100,11 @@
     moment_two = 0.999 * second_moment + 0.001 * mine * mine
     adam = moment_one / (jnp.sqrt(moment_two) + 1e-08)
     adam_sq, dir_sq = lax.psum(
-        (jnp.sum(adam * adam, axis=(1, 2)), jnp.sum(direction * direction, axis=(1, 2))),
-        ("tensor", "section"),
+        lax.psum(
+            (jnp.sum(adam * adam, axis=(1, 2)), jnp.sum(direction * direction, axis=(1, 2))),
+            "section",
+        ),
+        "tensor",
     )
     graft = jnp.sqrt(adam_sq) / (jnp.sqrt(dir_sq) + 1e-06)
     mask = valid[:, None, None]

time: 414 us -> 400 us (0.966)
  blocking collectives: 30.8 us -> 15.9 us
    psum x1, blocking collectives: 30.8 us -> 6.05 us  [on_device(): lax.psum((jnp.sum(adam * adam, axis=(1, 2)), jnp.sum(direction * directio...]
    psum x0 -> x1, blocking collectives: none -> 9.87 us  [on_device(): lax.psum(lax.psum((jnp.sum(adam * adam, axis=(1, 2)), jnp.sum(direction *...]
where the time goes in v1:
time: 400 us; the launch traced here: 399 us
  waiting for transfers between devices  291 us (73%)
  matrix products  30.6 us (8%)
  between operations  27.5 us (7%)
  local copies, waits for them, and re-layouts  21.3 us (5%)
  blocking collectives  15.9 us (4%)
  other arithmetic  12.2 us (3%)
    unnamed x6, waiting for transfers between devices  115 us
    all_gather x1, waiting for transfers between devices, on_device(): portion = lax.all_gather(mine, ('tensor', 'section'), axis=1, tiled=True)  65.6 us
    all_gather x1, waiting for transfers between devices, on_device(): lax.all_gather(right_root, ('tensor', 'section'), axis=1, tiled=True)  58.2 us
    psum x1, waiting for transfers between devices, on_device(): grad_rows = lax.psum(partial_rows, 'shard')  29.8 us
    psum x1, waiting for transfers between devices, spread(): return lax.psum(kept, axis)  22.6 us
    unnamed x32, local copies, waits for them, and re-layouts  13.4 us
    psum x1, blocking collectives, on_device(): lax.psum(lax.psum((jnp.sum(adam * adam, axis=(1, 2)), jnp.sum(direction *...  9.87 us
    dot_general x2, matrix products, absorb_slot(): block_part = jnp.dot(mine_rows, portion.T, precision=highest)  8.3 us
  transfers between devices with their start and end apart: 5, of which 5 were waited for; matrix products, arithmetic and copies ran while one was open for 6% of the time, Pallas kernels for 0%

profile of v1, /device:TPU:0, one launch (start us, length us, event | category | flops | bytes accessed | tf_op | source)
XLA Modules:
  0.0 399.0 jit_solution(17112780353811645618)
XLA Ops:
  7.2 2.4 fusion.108
  9.6 2.1 fusion.111
  13.4 4.1 %maximum_multiply_fusion = f32[768,3072]{0,1:T(8,128)} fusion(f32[768,768]{0,1:T(8,128)S(1)} %fusion.108, f32[768,768]{0,1:T(8,128)S(1)} %fusion.111, f32[768,768]{0,1:T(8,128)S(1)} %fusion.114, f32[768,768]{0,1:T(8,128)S(1)} %fusion.117), kind=kLoop, calls=%fused_computation.86 | loop fusion | flops 9437184 | bytes 18874368 | tf_op jit(solution)/shard_map/mul | solution.py:51
  17.5 9.7 %copy.20 = f32[768,3072]{1,0:T(8,128)} copy(f32[768,3072]{0,1:T(8,128)} %maximum_multiply_fusion) | data formatting | bytes 18874368
  27.2 114.2 %reduce-scatter.4.cloned.1.call-done = f32[48,3072]{1,0:T(8,128)} async-done(((f32[768,3072]{1,0:T(8,128)}), f32[48,3072]{1,0:T(8,128)}) %reduce-scatter.4.cloned.1.call-update) | async-done | bytes 589840
  141.4 1.5 copy.21
  142.9 1.3 copy.17
  144.4 29.8 %all-reduce.6.cloned.1.call-done = f32[48,4,768]{2,0,1:T(8,128)} async-done(((f32[48,4,768]{2,0,1:T(8,128)}), f32[48,4,768]{2,0,1:T(8,128)}) %all-reduce.6.cloned.1.call-update) | async-done | bytes 589840 | tf_op jit(solution)/shard_map/psum | solution.py:56
  174.2 1.6 gather_fusion.1
  175.9 1.2 fusion.134
  193.1 65.6 %all-gather.5.cloned.1.call-done = f32[4,768,768]{2,1,0:T(8,128)} async-done(((f32[4,48,768]{2,1,0:T(8,128)}), f32[4,768,768]{2,1,0:T(8,128)}) %all-gather.5.cloned.1.call-update) | async-done | bytes 9437200 | tf_op jit(solution)/shard_map/all_gather | solution.py:67
  258.8 11.2 %conditional.10 = (f32[48,768]{1,0:T(8,128)S(1)}, f32[1,48,768]{2,1,0:T(8,128)S(1)}, f32[1,48,768]{2,1,0:T(8,128)S(1)}) conditional(s32[]{:T(128)} %bitcast.42, () %tuple.93, (f32[4,48,768]{2,1,0:T(8,128)}, f32[4,768,768]{2,1,0:T(8,128)}, f32[4,48,768]{2,1,0:T(8,128)}, s32[]{:T(128)}) %tuple.90), branch_computations={%region_10.11_spmd, %region_11.12_spmd} | conditional | flops 1019215872 | bytes 12927038 | solution.py:73
  259.0 1.8 slice.65
  260.8 1.7 fusion.36
  262.5 3.3 fusion.31
  265.7 4.2 %fusion.33 = f32[1,48,768]{2,1,0:T(8,128)S(1)} fusion(f32[4,48,768]{2,1,0:T(8,128)} %get-tuple-element.80, f32[4,768,768]{2,1,0:T(8,128)} %get-tuple-element.79), kind=kOutput, calls=%fused_computation.29 | convolution fusion | flops 339738624 | bytes 2654208 | tf_op jit(solution)/shard_map/cond/branch_1_fun/dot_general | solution.py:16
  271.4 10.8 %conditional.14 = (f32[48,768]{1,0:T(8,128)S(1)}, f32[1,48,768]{2,1,0:T(8,128)S(1)}, f32[1,48,768]{2,1,0:T(8,128)S(1)}) conditional(s32[]{:T(128)} %bitcast.44, () %tuple.99, (f32[4,48,768]{2,1,0:T(8,128)}, f32[4,768,768]{2,1,0:T(8,128)}, f32[4,48,768]{2,1,0:T(8,128)}, s32[]{:T(128)}) %tuple.90), branch_computations={%region_18.19_spmd, %region_19.20_spmd} | conditional | flops 1019215872 | bytes 12927038 | solution.py:73
  271.4 1.8 slice.73
  273.3 1.7 fusion.90
  274.9 3.3 fusion.85
  278.2 4.0 %fusion.87 = f32[1,48,768]{2,1,0:T(8,128)S(1)} fusion(f32[4,48,768]{2,1,0:T(8,128)} %get-tuple-element.92, f32[4,768,768]{2,1,0:T(8,128)} %get-tuple-element.91), kind=kOutput, calls=%fused_computation.71 | convolution fusion | flops 339738624 | bytes 2654208 | tf_op jit(solution)/shard_map/cond/branch_1_fun/dot_general | solution.py:16
  282.3 58.2 %all-gather.3.cloned.1.call-done = f32[4,768,768]{2,1,0:T(8,128)} async-done(((f32[4,48,768]{2,1,0:T(8,128)}), f32[4,768,768]{2,1,0:T(8,128)}) %all-gather.3.cloned.1.call-update) | async-done | bytes 9437200 | tf_op jit(solution)/shard_map/all_gather | solution.py:87
  340.5 3.2 conditional.11
  340.5 3.2 fusion.51
  343.8 0.8 copy-done.13
  344.6 3.2 conditional.15
  344.6 3.2 fusion.105
  348.0 3.3 fusion.133
  351.3 6.0 %all-reduce = (f32[4]{0:T(128)S(1)}, f32[4]{0:T(128)S(1)}) all-reduce(f32[4]{0:T(128)S(1)} %multiply_reduce_fusion, f32[4]{0:T(128)S(1)} %get-tuple-element.142), channel_id=1, replica_groups=mesh['shard'=2,'tensor'=4,'section'=4] {'section'}, use_global_device_ids=true, to_apply=%region_23.24 | all-reduce | flops 8 | bytes 64 | tf_op jit(solution)/shard_map/psum | solution.py:103
  357.3 9.9 %all-reduce.1 = (f32[4]{0:T(128)S(1)}, f32[4]{0:T(128)S(1)}) all-reduce(f32[4]{0:T(128)S(1)} %get-tuple-element.129, f32[4]{0:T(128)S(1)} %get-tuple-element.130), channel_id=1, replica_groups=mesh['shard'=2,'tensor'=4,'section'=4] {'tensor'}, use_global_device_ids=true, to_apply=%region_24.25 | all-reduce | flops 8 | bytes 64 | tf_op jit(solution)/shard_map/psum | solution.py:102
  368.1 22.6 %all-reduce.8.cloned.1.call-done = (bf16[1,48,768]{2,1,0:T(8,128)(2,1)}, bf16[1,48,768]{2,1,0:T(8,128)(2,1)}, bf16[1,48,768]{2,1,0:T(8,128)(2,1)}, bf16[1,48,768]{2,1,0:T(8,128)(2,1)}) async-done(((bf16[1,48,768]{2,1,0:T(8,128)(2,1)}, bf16[1,48,768]{2,1,0:T(8,128)(2,1)}, bf16[1,48,768]{2,1,0:T(8,128)(2,1)}, bf16[1,48,768]{2,1,0:T(8,128)(2,1)}), (bf16[1,48,768]{2,1,0:T(8,128)(2,1)}, ...) | async-done | bytes 294928 | tf_op jit(solution)/shard_map/psum | solution.py:10
  390.7 1.7 pad_maximum_fusion.1
  (62 shorter events, 7.3 us)
Async XLA Ops:
  7.2 185.2 %copy-start = (bf16[4,48,768]{2,1,0:T(8,128)(2,1)S(1)}, bf16[4,48,768]{2,1,0:T(8,128)(2,1)}, u32[]{:S(2)}) copy-start(bf16[4,48,768]{2,1,0:T(8,128)(2,1)} %param.28) | copy-start | bytes 884740
  7.2 2.4 copy-start.3
  7.2 134.2 %reduce-scatter.4.cloned.1.call-start = ((), (), s32[]{:S(2)}) async-start(), calls=%async_computation.4 | async-start | bytes 10027008
  9.6 2.1 copy-start.4
  27.2 117.1 %copy-start.14 = (s32[8]{0:T(128)S(1)}, s32[8]{0:T(128)}, u32[]{:S(2)}) copy-start(s32[8]{0:T(128)} %param.29) | copy-start | bytes 100
  27.2 147.0 %all-reduce.6.cloned.1.call-start = ((), (), s32[]{:S(2)}) async-start(), calls=%async_computation.1 | async-start | bytes 1179648 | tf_op jit(solution)/shard_map/psum | solution.py:56
  142.9 32.9 %copy-start.5 = (f32[4,48,768]{2,1,0:T(8,128)S(1)}, f32[4,48,768]{2,1,0:T(8,128)}, u32[]{:S(2)}) copy-start(f32[4,48,768]{2,1,0:T(8,128)} %param.35) | copy-start | bytes 1769476
  144.2 114.5 %all-gather.5.cloned.1.call-start = ((), (), s32[]{:S(2)}) async-start(), calls=%async_computation.3 | async-start | bytes 10027008 | tf_op jit(solution)/shard_map/all_gather | solution.py:67
  177.1 163.4 %all-gather.3.cloned.1.call-start = ((), (), s32[]{:S(2)}) async-start(), calls=%async_computation.2 | async-start | bytes 10027008 | tf_op jit(solution)/shard_map/all_gather | solution.py:87
  177.7 213.1 %all-reduce.8.cloned.1.call-start = ((), (), s32[]{:S(2)}) async-start(), calls=%async_computation.5 | async-start | bytes 589824 | tf_op jit(solution)/shard_map/psum | solution.py:10
  270.0 0.7 copy-start.7
  270.7 0.7 copy-start.8
  270.7 0.7 copy-start.9
  282.3 61.4 %copy-start.10 = (f32[1,48,768]{2,1,0:T(8,128)}, f32[1,48,768]{2,1,0:T(8,128)S(1)}, u32[]{:S(2)}) copy-start(f32[1,48,768]{2,1,0:T(8,128)S(1)} %get-tuple-element.120) | copy-start | bytes 442372
  282.3 61.4 %copy-start.11 = (f32[1,48,768]{2,1,0:T(8,128)}, f32[1,48,768]{2,1,0:T(8,128)S(1)}, u32[]{:S(2)}) copy-start(f32[1,48,768]{2,1,0:T(8,128)S(1)} %get-tuple-element.124) | copy-start | bytes 442372
  282.3 61.4 %copy-start.12 = (f32[48,768]{1,0:T(8,128)}, f32[48,768]{1,0:T(8,128)S(1)}, u32[]{:S(2)}) copy-start(f32[48,768]{1,0:T(8,128)S(1)} %get-tuple-element.116) | copy-start | bytes 442372
  343.7 0.9 copy-start.13
  343.8 4.2 %copy-start.2 = (f32[4,48,768]{2,1,0:T(8,128)S(1)}, f32[4,48,768]{2,1,0:T(8,128)}, u32[]{:S(2)}) copy-start(f32[4,48,768]{2,1,0:T(8,128)} %get-tuple-element.138) | copy-start | bytes 1769476
  343.8 4.2 %copy-start.6 = (f32[4,48,768]{2,1,0:T(8,128)S(1)}, f32[4,48,768]{2,1,0:T(8,128)}, u32[]{:S(2)}) copy-start(f32[4,48,768]{2,1,0:T(8,128)} %param.34) | copy-start | bytes 1769476
  348.0 44.5 %copy-start.1 = (bf16[4,48,768]{2,1,0:T(8,128)(2,1)S(1)}, bf16[4,48,768]{2,1,0:T(8,128)(2,1)}, u32[]{:S(2)}) copy-start(bf16[4,48,768]{2,1,0:T(8,128)(2,1)} %param.28) | copy-start | bytes 884740
Sparse Core Ops, SparseCore 0:
  27.3 114.0 reduce-scatter.3
  144.4 29.7 all-reduce.5
  177.2 81.4 all-gather.4
  260.8 79.5 all-gather.2
  368.3 22.4 all-reduce.7
